TPU v7x, 32 devices: a whole 2x2x4 slice. The times are simulated.
32 devices in a mesh: db: 8 (over z, x), pb: 4 (over y, core).
Axes of the slice: x: 2, y: 2, z: 4, core: 2. Of those that a mesh axis runs over, the one named last changes fastest.
Arguments:
- queries: bfloat16 [256, 4096], P('pb'), may hold values from -6 to 6
- database: bfloat16 [8192, 4096], P(('db', 'pb')), may hold values from -6 to 6
- slopes: int32 [5], replicated, may hold values from 1 to 6, as said below
Outputs:
- match_score: float32 [256, 8192], P(None, ('db', 'pb'))
Inputs may be any that keep to these rules, and one draw needn't show every extreme that they name: `slopes`: every slope lies in 1 to 6; one of them is 6 and one is 1.
All inputs are finite; a program needn't handle non-finite values.
Results may differ from a plain program's by a relative error of at most 0.0003.
Values may be sent and summed in bfloat16 or wider, within the bound.
A program may use at most 64 MiB of HBM per device.

v0:
```python
import jax
import jax.numpy as jnp
from jax import lax
from jax.sharding import PartitionSpec as P

SEQ = 20
RADIUS = 5
SLOPES = 5
SMAX = 6
variance_floor = 0.25


def padded_2(value, sides, width):
    for axis, dim in sides:
        count, length = (lax.axis_size(axis), value.shape[dim])
        up = [(i, (i + 1) % count) for i in range(count - 1)]
        down = [(j, i) for i, j in up]
        last = lax.slice_in_dim(value, length - width, length, axis=dim)
        leading = lax.slice_in_dim(value, 0, width, axis=dim)
        before = lax.ppermute(last, axis, up)
        after = lax.ppermute(leading, axis, down)
        value = jnp.concatenate([before, value, after], axis=dim)
    return value


def from_behind(value, axis, steps):
    count = lax.axis_size(axis)
    leading, last = (max(0, -steps), min(count, count - steps))
    return lax.ppermute(value, axis, [(source, source + steps) for source in range(leading, last)])


def band_mask(first_frame, frame_count, band_total):
    frame_ids = first_frame + jnp.arange(frame_count, dtype=jnp.int32)
    inside = jnp.logical_and(frame_ids >= 0, frame_ids < band_total)
    return inside.astype(jnp.float32)[None, :]


def contrast(extended, validity):
    out_width = extended.shape[1] - 2 * RADIUS
    masked = extended * validity
    squared = masked * masked
    first_sum = masked[:, :out_width]
    second_sum = squared[:, :out_width]
    counted = validity[:, :out_width]
    for offset in range(1, 2 * RADIUS + 1):
        first_sum = first_sum + masked[:, offset : offset + out_width]
        second_sum = second_sum + squared[:, offset : offset + out_width]
        counted = counted + validity[:, offset : offset + out_width]
    counted = jnp.maximum(counted, 1.0)
    average = first_sum / counted
    spread = second_sum / counted - average * average
    center = extended[:, RADIUS : RADIUS + out_width]
    keeper = validity[:, RADIUS : RADIUS + out_width]
    return keeper * (center - average) / jnp.sqrt(jnp.maximum(spread, variance_floor))


def lagged(field, steps, slope):
    col_pad = steps * SMAX
    padded = jnp.pad(field, ((steps, 0), (col_pad, 0)))
    begin = col_pad - steps * slope
    return lax.dynamic_slice(padded, (jnp.int32(0), begin), field.shape)


def window_sum(field, slope):
    powers = [field]
    stride = 1
    while 2 * stride <= SEQ:
        powers.append(powers[-1] + lagged(powers[-1], stride, slope))
        stride = stride * 2
    summed = None
    filled = 0
    for level in reversed(range(len(powers))):
        if SEQ >> level & 1:
            segment = powers[level] if filled == 0 else lagged(powers[level], filled, slope)
            summed = segment if summed is None else summed + segment
            filled = filled + (1 << level)
    return summed


def best_match(joined, slopes, reach):
    highest = None
    for member in range(SLOPES):
        summed = window_sum(joined, slopes[member])[:, reach:]
        highest = summed if highest is None else jnp.maximum(highest, summed)
    return highest * SEQ ** (-0.5)


def on_device(queries, database, slopes):
    frames = database.shape[0]
    scale = database.shape[1] ** (-0.5)
    reach = SMAX * (SEQ - 1)
    band_total = frames * lax.axis_size(("db", "pb"))
    similarity = (
        lax.dot_general(
            lax.all_gather(queries, "pb", axis=0, tiled=True),
            database,
            (((1,), (1,)), ((), ())),
            preferred_element_type=jnp.float32,
        )
        * scale
    )
    anchor = lax.axis_index(("db", "pb")) * frames
    extended = padded_2(similarity, ((("db", "pb"), 1),), RADIUS)
    normed = contrast(extended, band_mask(anchor - RADIUS, frames + 2 * RADIUS, band_total))
    carried = from_behind(normed[:, frames - reach :], ("db", "pb"), 1)
    joined = jnp.concatenate([carried, normed], axis=1)
    return best_match(joined, slopes, reach)


def solution(mesh):
    placed = (P("pb", None), P(("db", "pb"), None), P())
    return jax.shard_map(
        on_device, mesh=mesh, in_specs=placed, out_specs=P(None, ("db", "pb")), check_vma=False
    )
```

profile of v0, /device:TPU:7, one launch (start us, length us, event | category | flops | bytes accessed | tf_op | source)
XLA Modules:
  0.0 78.5 jit_solution(4593972485175373865)
XLA Ops:
  6.5 0.0 copy-start
  6.5 0.0 all-gather.2.cloned.1.call-start
  6.5 0.7 all-gather.2.cloned.1.call-update
  7.3 0.1 fusion.44
  7.4 24.8 %all-gather.2.cloned.1.call-done = bf16[256,4096]{1,0:T(8,128)(2,1)} async-done(((bf16[64,4096]{1,0:T(8,128)(2,1)}), bf16[256,4096]{1,0:T(8,128)(2,1)}) %all-gather.2.cloned.1.call-update) | async-done | bytes 2097168 | tf_op jit(solution)/shard_map/all_gather | solution.py:95
  32.2 0.0 copy-done
  32.2 2.3 %convolution_multiply_fusion = f32[256,256]{0,1:T(8,128)S(1)} fusion(bf16[256,4096]{1,0:T(8,128)(2,1)} %all-gather.2.cloned.1.call-done, bf16[256,4096]{1,0:T(8,128)(2,1)S(1)} %copy-done), kind=kOutput, calls=%fused_computation | convolution fusion | flops 536936448 | bytes 4456448 | tf_op jit(solution)/shard_map/dot_general | solution.py:94
  34.6 4.2 %collective-permute-start = (f32[256,5]{0,1:T(8,128)S(1)}, f32[256,5]{0,1:T(8,128)S(1)}, u32[]{:S(2)}, u32[]{:S(2)}) collective-permute-start(f32[256,5]{0,1:T(8,128)S(1)} %get-tuple-element.12), channel_id=1, source_target_pairs={{0,1},{1,2},{2,3},{3,4},{4,5},{5,6},{6,7},{7,8},{8,9},{9,10},{10,1... | collective-permute-start | bytes 15368 | tf_op jit(solution)/shard_map/ppermute | solution.py:20
  38.7 1.9 %collective-permute-start.1 = (f32[256,5]{0,1:T(8,128)S(1)}, f32[256,5]{0,1:T(8,128)S(1)}, u32[]{:S(2)}, u32[]{:S(2)}) collective-permute-start(f32[256,5]{0,1:T(8,128)S(1)} %get-tuple-element.13), channel_id=1, source_target_pairs={{1,0},{2,1},{3,2},{4,3},{5,4},{6,5},{7,6},{8,7},{9,8},{10,9},{11,1... | collective-permute-start | bytes 15368 | tf_op jit(solution)/shard_map/ppermute | solution.py:21
  40.7 0.0 collective-permute-done
  40.7 4.8 %collective-permute-done.1 = f32[256,5]{0,1:T(8,128)S(1)} collective-permute-done((f32[256,5]{0,1:T(8,128)S(1)}, f32[256,5]{0,1:T(8,128)S(1)}, u32[]{:S(2)}, u32[]{:S(2)}) %collective-permute-start.1) | collective-permute-done | bytes 5152 | tf_op jit(solution)/shard_map/ppermute | solution.py:21
  45.5 0.1 fusion.42
  45.6 0.0 copy-start.1
  45.6 0.5 fusion.34
  46.2 1.9 %collective-permute-start.2 = (f32[256,114]{0,1:T(8,128)S(1)}, f32[256,114]{0,1:T(8,128)S(1)}, u32[]{:S(2)}, u32[]{:S(2)}) collective-permute-start(f32[256,114]{0,1:T(8,128)S(1)} %slice.220), channel_id=1, source_target_pairs={{0,1},{1,2},{2,3},{3,4},{4,5},{5,6},{6,7},{7,8},{8,9},{9,10},{10,1... | collective-permute-start | bytes 350216 | tf_op jit(solution)/shard_map/ppermute | solution.py:29
  48.1 0.0 copy-done.1
  48.2 0.7 fusion.45
  67.1 0.0 collective-permute-done.2
  67.1 0.7 fusion.14
  67.8 0.2 fusion.4
  68.0 0.2 fusion.9
  68.2 0.3 fusion.2
  68.5 0.2 fusion.7
  68.7 0.2 fusion.8
  68.9 0.3 fusion
  69.2 0.2 fusion.5
  69.4 0.2 fusion.6
  69.6 1.2 %fusion.21 = f32[256,256]{0,1:T(8,128)S(1)} fusion(s32[]{:T(128)S(6)} %add.489, f32[256,370]{0,1:T(8,128)S(1)} %fusion.5, s32[]{:T(128)S(6)} %add.491, f32[256,370]{0,1:T(8,128)S(1)} %fusion.6, s32[]{:T(128)S(6)} %add.493, f32[256,370]{0,1:T(8,128)S(1)} %fusion.7, s32[]{:T(128)S(6)} %add.495, f32[256,370]{0,1:T(8,128)S(1)} %fusion.8, s32[]{:T(128)S(6)} %add.497, ...), kind=kLoop, calls=%fused_computation.49 | loop fusion | flops 983040 | bytes 5423144 | tf_op jit(solution)/shard_map/mul | solution.py:85
  70.8 0.8 %copy.4 = f32[256,256]{1,0:T(8,128)} copy(f32[256,256]{0,1:T(8,128)S(1)} %fusion.21) | data formatting | bytes 524288 | tf_op jit(solution)/shard_map/mul | solution.py:85
  (5 shorter events, 0.1 us)
Async XLA Ops:
  6.5 25.7 %copy-start = (bf16[256,4096]{1,0:T(8,128)(2,1)S(1)}, bf16[256,4096]{1,0:T(8,128)(2,1)}, u32[]{:S(2)}) copy-start(bf16[256,4096]{1,0:T(8,128)(2,1)} %param.4) | copy-start | bytes 6291460
  6.5 25.7 %all-gather.2.cloned.1.call-start = ((), (), s32[]{:S(2)}) async-start(), calls=%async_computation | async-start | bytes 2621440 | tf_op jit(solution)/shard_map/all_gather | solution.py:95
  34.6 6.1 %collective-permute-start = (f32[256,5]{0,1:T(8,128)S(1)}, f32[256,5]{0,1:T(8,128)S(1)}, u32[]{:S(2)}, u32[]{:S(2)}) collective-permute-start(f32[256,5]{0,1:T(8,128)S(1)} %get-tuple-element.12), channel_id=1, source_target_pairs={{0,1},{1,2},{2,3},{3,4},{4,5},{5,6},{6,7},{7,8},{8,9},{9,10},{10,1... | collective-permute-start | bytes 15368 | tf_op jit(solution)/shard_map/ppermute | solution.py:20
  38.7 6.8 %collective-permute-start.1 = (f32[256,5]{0,1:T(8,128)S(1)}, f32[256,5]{0,1:T(8,128)S(1)}, u32[]{:S(2)}, u32[]{:S(2)}) collective-permute-start(f32[256,5]{0,1:T(8,128)S(1)} %get-tuple-element.13), channel_id=1, source_target_pairs={{1,0},{2,1},{3,2},{4,3},{5,4},{6,5},{7,6},{8,7},{9,8},{10,9},{11,1... | collective-permute-start | bytes 15368 | tf_op jit(solution)/shard_map/ppermute | solution.py:21
  45.6 2.5 %copy-start.1 = (s32[5]{0:T(128)S(1)}, s32[5]{0:T(128)}, u32[]{:S(2)}) copy-start(s32[5]{0:T(128)} %param.5) | copy-start | bytes 64
  46.2 20.9 %collective-permute-start.2 = (f32[256,114]{0,1:T(8,128)S(1)}, f32[256,114]{0,1:T(8,128)S(1)}, u32[]{:S(2)}, u32[]{:S(2)}) collective-permute-start(f32[256,114]{0,1:T(8,128)S(1)} %slice.220), channel_id=1, source_target_pairs={{0,1},{1,2},{2,3},{3,4},{4,5},{5,6},{6,7},{7,8},{8,9},{9,10},{10,1... | collective-permute-start | bytes 350216 | tf_op jit(solution)/shard_map/ppermute | solution.py:29
Sparse Core Ops, SparseCore 0:
  8.9 23.2 all-gather.1
where the time goes:
time: 78.9 us; the launch traced here: 78.5 us
  between operations  31.8 us (40%)
  waiting for transfers between devices  30.4 us (39%)
  starting transfers between devices  8.05 us (10%)
  other arithmetic  4.36 us (6%)
  matrix products  2.33 us (3%)
  local copies, waits for them, and re-layouts  1.52 us (2%)
    all_gather x1, waiting for transfers between devices, on_device(): lax.all_gather(queries, 'pb', axis=0, tiled=True)  24.8 us
    ppermute x1, waiting for transfers between devices, padded_2(): after = lax.ppermute(leading, axis, down)  4.81 us
    ppermute x1, starting transfers between devices, padded_2(): before = lax.ppermute(last, axis, up)  4.18 us
    add x9, other arithmetic, window_sum(): powers.append(powers[-1] + lagged(powers[-1], stride, slope))  2.43 us
    dot_general x1, matrix products, on_device(): lax.dot_general(lax.all_gather(queries, 'pb', axis=0, tiled=True), databa...  2.33 us
    ppermute x1, starting transfers between devices, from_behind(): lax.ppermute(value, axis, [(source, source + steps) for source in range(l...  1.94 us
    ppermute x1, starting transfers between devices, padded_2(): after = lax.ppermute(leading, axis, down)  1.92 us
  transfers between devices with their start and end apart: 4, of which 2 were waited for; matrix products, arithmetic and copies ran while one was open for 1% of the time, Pallas kernels for 0%

commit v1 on v0

--- a/solution.py
+++ b/solution.py
@@ -90,9 +90,30 @@
     scale = database.shape[1] ** (-0.5)
     reach = SMAX * (SEQ - 1)
     band_total = frames * lax.axis_size(("db", "pb"))
+
+    def edit_trees(own_rows, ax_name):
+        passed, t1, v_next = (
+            jax.lax.axis_size(ax_name),
+            jax.lax.axis_index(ax_name),
+            own_rows.shape[0],
+        )
+        views = [(rr, (rr + 1) % passed) for rr in range(passed)]
+        so_far_all = [(rr, (rr - 1) % passed) for rr in range(passed)]
+        z = jnp.zeros((*own_rows.shape[:0], passed * v_next, *own_rows.shape[1:]), own_rows.dtype)
+        z = lax.dynamic_update_slice_in_dim(z, own_rows, t1 * v_next, axis=0)
+        local_now = lower = own_rows
+        earlier = passed // 2
+        for w in tuple(range(1, earlier + 1)):
+            local_now = jax.lax.ppermute(local_now, ax_name, perm=views)
+            z = lax.dynamic_update_slice_in_dim(z, local_now, (t1 - w) % passed * v_next, axis=0)
+            if w < passed - earlier:
+                lower = jax.lax.ppermute(lower, axis_name=ax_name, perm=so_far_all)
+                z = lax.dynamic_update_slice_in_dim(z, lower, (t1 + w) % passed * v_next, axis=0)
+        return z
+
     similarity = (
         lax.dot_general(
-            lax.all_gather(queries, "pb", axis=0, tiled=True),
+            edit_trees(queries, "pb"),
             database,
             (((1,), (1,)), ((), ())),
             preferred_element_type=jnp.float32,

time: 78.9 us -> 62.9 us (0.80)
  the two profiles are of different devices: /device:TPU:7 before, /device:TPU:0 now
where the time goes in v1:
time: 62.9 us; the launch traced here: 62.4 us
  between operations  18.7 us (30%)
  starting transfers between devices  15 us (24%)
  waiting for transfers between devices  14.5 us (23%)
  local copies, waits for them, and re-layouts  7.49 us (12%)
  other arithmetic  4.34 us (7%)
  matrix products  2.33 us (4%)
    ppermute x2, waiting for transfers between devices, edit_trees(): local_now = jax.lax.ppermute(local_now, ax_name, perm=views)  10.8 us
    ppermute x1, starting transfers between devices, padded_2(): before = lax.ppermute(last, axis, up)  4.35 us
    ppermute x1, starting transfers between devices, from_behind(): lax.ppermute(value, axis, [(source, source + steps) for source in range(l...  4.31 us
    ppermute x1, waiting for transfers between devices, padded_2(): after = lax.ppermute(leading, axis, down)  3.71 us
    ppermute x2, starting transfers between devices, edit_trees(): local_now = jax.lax.ppermute(local_now, ax_name, perm=views)  3.02 us
    add x9, other arithmetic, window_sum(): powers.append(powers[-1] + lagged(powers[-1], stride, slope))  2.41 us
    dot_general x1, matrix products, on_device(): lax.dot_general(edit_trees(queries, 'pb'), database, (((1,), (1,)), ((),...  2.33 us
    ppermute x1, starting transfers between devices, edit_trees(): lower = jax.lax.ppermute(lower, axis_name=ax_name, perm=so_far_all)  2.01 us
  transfers between devices with their start and end apart: 6, of which 3 were waited for; matrix products, arithmetic and copies ran while one was open for 9% of the time, Pallas kernels for 0%

profile of v1, /device:TPU:0, one launch (start us, length us, event | category | flops | bytes accessed | tf_op | source)
XLA Modules:
  0.0 62.4 jit_solution(13298797206060666680)
XLA Ops:
  0.0 0.0 copy-start
  0.0 0.0 copy-start.1
  0.0 0.5 collective-permute-start
  0.5 2.0 %collective-permute-start.1 = (bf16[64,4096]{1,0:T(8,128)(2,1)}, bf16[64,4096]{1,0:T(8,128)(2,1)}, u32[]{:S(2)}, u32[]{:S(2)}) collective-permute-start(bf16[64,4096]{1,0:T(8,128)(2,1)} %param.3), channel_id=1, source_target_pairs={{0,3},{1,0},{2,1},{3,2},{4,7},{5,4},{6,5},{7,6},{8,11},{9,8},{10,9... | collective-permute-start | bytes 1572872 | tf_op jit(solution)/shard_map/ppermute | solution.py:110
  2.5 1.6 %broadcast_in_dim.4 = bf16[256,4096]{1,0:T(8,128)(2,1)} broadcast(bf16[]{:T(256)} %constant.156.clone.1), dimensions={} | broadcast | bytes 2097154 | tf_op jit(solution)/shard_map/broadcast_in_dim | solution.py:102
  4.1 0.0 copy-done.1
  4.1 0.8 %constant_dynamic-update-slice_fusion.3 = bf16[256,4096]{1,0:T(8,128)(2,1)} fusion(bf16[256,4096]{1,0:T(8,128)(2,1)} %broadcast_in_dim.4, bf16[64,4096]{1,0:T(8,128)(2,1)S(1)} %copy-done.1, s32[]{:T(128)S(6)} %select_n.102), kind=kLoop, calls=%fused_computation.87 | loop fusion | bytes 1048580 | tf_op jit(solution)/shard_map/dynamic_update_slice | solution.py:103
  4.9 0.1 fusion.44
  5.0 7.5 %collective-permute-done = bf16[64,4096]{1,0:T(8,128)(2,1)S(1)} collective-permute-done((bf16[64,4096]{1,0:T(8,128)(2,1)}, bf16[64,4096]{1,0:T(8,128)(2,1)S(1)}, u32[]{:S(2)}, u32[]{:S(2)}) %collective-permute-start) | collective-permute-done | bytes 524320 | tf_op jit(solution)/shard_map/ppermute | solution.py:107
  12.5 2.6 %collective-permute-start.2 = (bf16[64,4096]{1,0:T(8,128)(2,1)S(1)}, bf16[64,4096]{1,0:T(8,128)(2,1)S(1)}, u32[]{:S(2)}, u32[]{:S(2)}) collective-permute-start(bf16[64,4096]{1,0:T(8,128)(2,1)S(1)} %collective-permute-done), channel_id=1, source_target_pairs={{0,1},{1,2},{2,3},{3,0},{4,5},{5,6},{6,7},{7,4},{8,9},{9,10},{10,1... | collective-permute-start | bytes 1572872 | tf_op jit(solution)/shard_map/ppermute | solution.py:107
  15.1 0.8 %constant_dynamic-update-slice_fusion.2 = bf16[256,4096]{1,0:T(8,128)(2,1)} fusion(bf16[256,4096]{1,0:T(8,128)(2,1)} %constant_dynamic-update-slice_fusion.3, bf16[64,4096]{1,0:T(8,128)(2,1)S(1)} %collective-permute-done, s32[]{:T(128)S(6)} %select_n.104), kind=kLoop, calls=%fused_computation.86 | loop fusion | bytes 1048580 | tf_op jit(solution)/shard_map/dynamic_update_slice | solution.py:108
  15.9 0.0 collective-permute-done.1
  15.9 1.9 %constant_dynamic-update-slice_fusion.1 = bf16[256,4096]{1,0:T(8,128)(2,1)} fusion(bf16[256,4096]{1,0:T(8,128)(2,1)} %constant_dynamic-update-slice_fusion.2, bf16[64,4096]{1,0:T(8,128)(2,1)} %collective-permute-done.1, s32[]{:T(128)S(6)} %select_n.106), kind=kLoop, calls=%fused_computation.85 | loop fusion | bytes 1048580 | tf_op jit(solution)/shard_map/dynamic_update_slice | solution.py:111
  17.8 3.3 %collective-permute-done.2 = bf16[64,4096]{1,0:T(8,128)(2,1)S(1)} collective-permute-done((bf16[64,4096]{1,0:T(8,128)(2,1)S(1)}, bf16[64,4096]{1,0:T(8,128)(2,1)S(1)}, u32[]{:S(2)}, u32[]{:S(2)}) %collective-permute-start.2) | collective-permute-done | bytes 524320 | tf_op jit(solution)/shard_map/ppermute | solution.py:107
  21.1 0.9 %constant_dynamic-update-slice_fusion = bf16[256,4096]{1,0:T(8,128)(2,1)} fusion(bf16[256,4096]{1,0:T(8,128)(2,1)} %constant_dynamic-update-slice_fusion.1, bf16[64,4096]{1,0:T(8,128)(2,1)S(1)} %collective-permute-done.2, s32[]{:T(128)S(6)} %select_n.108), kind=kLoop, calls=%fused_computation.84 | loop fusion | bytes 1048580 | tf_op jit(solution)/shard_map/dynamic_update_slice | solution.py:108
  22.0 0.0 copy-done
  22.0 2.3 %convolution_multiply_fusion = f32[256,256]{0,1:T(8,128)S(1)} fusion(bf16[256,4096]{1,0:T(8,128)(2,1)} %constant_dynamic-update-slice_fusion, bf16[256,4096]{1,0:T(8,128)(2,1)S(1)} %copy-done), kind=kOutput, calls=%fused_computation | convolution fusion | flops 536936448 | bytes 4456448 | tf_op jit(solution)/shard_map/dot_general | solution.py:115
  24.3 4.3 %collective-permute-start.3 = (f32[256,5]{0,1:T(8,128)S(1)}, f32[256,5]{0,1:T(8,128)S(1)}, u32[]{:S(2)}, u32[]{:S(2)}) collective-permute-start(f32[256,5]{0,1:T(8,128)S(1)} %get-tuple-element.12), channel_id=1, source_target_pairs={{0,1},{1,2},{2,3},{3,4},{4,5},{5,6},{6,7},{7,8},{8,9},{9,10},{10,1... | collective-permute-start | bytes 15368 | tf_op jit(solution)/shard_map/ppermute | solution.py:20
  28.7 1.3 %collective-permute-start.4 = (f32[256,5]{0,1:T(8,128)S(1)}, f32[256,5]{0,1:T(8,128)S(1)}, u32[]{:S(2)}, u32[]{:S(2)}) collective-permute-start(f32[256,5]{0,1:T(8,128)S(1)} %get-tuple-element.13), channel_id=1, source_target_pairs={{1,0},{2,1},{3,2},{4,3},{5,4},{6,5},{7,6},{8,7},{9,8},{10,9},{11,1... | collective-permute-start | bytes 15368 | tf_op jit(solution)/shard_map/ppermute | solution.py:21
  30.0 0.0 collective-permute-done.3
  30.0 3.7 %collective-permute-done.4 = f32[256,5]{0,1:T(8,128)S(1)} collective-permute-done((f32[256,5]{0,1:T(8,128)S(1)}, f32[256,5]{0,1:T(8,128)S(1)}, u32[]{:S(2)}, u32[]{:S(2)}) %collective-permute-start.4) | collective-permute-done | bytes 5152 | tf_op jit(solution)/shard_map/ppermute | solution.py:21
  33.7 0.1 fusion.42
  33.8 0.0 copy-start.2
  33.8 0.5 fusion.34
  34.4 4.3 %collective-permute-start.5 = (f32[256,114]{0,1:T(8,128)S(1)}, f32[256,114]{0,1:T(8,128)S(1)}, u32[]{:S(2)}, u32[]{:S(2)}) collective-permute-start(f32[256,114]{0,1:T(8,128)S(1)} %slice.220), channel_id=1, source_target_pairs={{0,1},{1,2},{2,3},{3,4},{4,5},{5,6},{6,7},{7,8},{8,9},{9,10},{10,1... | collective-permute-start | bytes 350216 | tf_op jit(solution)/shard_map/ppermute | solution.py:29
  38.7 0.0 copy-done.2
  38.7 0.6 %fusion.45 = (s32[1]{0:T(128)}, s32[1]{0:T(128)}, s32[1]{0:T(128)}, s32[1]{0:T(128)}, s32[1]{0:T(128)}) fusion(s32[5]{0:T(128)S(1)} %copy-done.2), kind=kLoop, calls=%fused_computation.108 | loop fusion | bytes 40 | tf_op jit(solution)/shard_map/slice | solution.py:83
  57.8 0.0 collective-permute-done.5
  57.9 0.6 %fusion.14 = (f32[256,370]{0,1:T(8,128)S(1)}, f32[256,370]{0,1:T(8,128)S(1)}, f32[256,370]{0,1:T(8,128)S(1)}, f32[256,370]{0,1:T(8,128)S(1)}, f32[256,370]{0,1:T(8,128)S(1)}) fusion(f32[256,370]{0,1:T(8,128)S(1)} %pad_maximum_fusion, s32[]{:T(128)S(6)} %select_n.129, s32[]{:T(128)S(6)} %select_n.124, s32[]{:T(128)S(6)} %select_n.119, s32[]{:T(128)S(6)} %select_n.114, ...), kind=kLoop, calls=%fused_computation.40 | loop fusion | flops 473600 | bytes 2273300 | tf_op jit(solution)/shard_map/add | solution.py:68
  58.5 0.3 fusion.2
  58.9 0.2 fusion.8
  59.1 0.2 fusion.7
  59.3 0.3 fusion
  59.6 0.2 fusion.6
  59.8 0.2 fusion.5
  60.0 0.2 fusion.4
  60.2 0.2 fusion.9
  60.3 1.2 %fusion.21 = f32[256,256]{0,1:T(8,128)S(1)} fusion(s32[]{:T(128)S(6)} %add.524, f32[256,370]{0,1:T(8,128)S(1)} %fusion.5, s32[]{:T(128)S(6)} %add.526, f32[256,370]{0,1:T(8,128)S(1)} %fusion.6, s32[]{:T(128)S(6)} %add.528, f32[256,370]{0,1:T(8,128)S(1)} %fusion.7, s32[]{:T(128)S(6)} %add.530, f32[256,370]{0,1:T(8,128)S(1)} %fusion.8, s32[]{:T(128)S(6)} %add.532, ...), kind=kLoop, calls=%fused_computation.49 | loop fusion | flops 983040 | bytes 5423144 | tf_op jit(solution)/shard_map/mul | solution.py:85
  61.5 0.8 %copy.4 = f32[256,256]{1,0:T(8,128)} copy(f32[256,256]{0,1:T(8,128)S(1)} %fusion.21) | data formatting | bytes 524288 | tf_op jit(solution)/shard_map/mul | solution.py:85
  (5 shorter events, 0.1 us)
Async XLA Ops:
  0.0 22.0 %copy-start = (bf16[256,4096]{1,0:T(8,128)(2,1)S(1)}, bf16[256,4096]{1,0:T(8,128)(2,1)}, u32[]{:S(2)}) copy-start(bf16[256,4096]{1,0:T(8,128)(2,1)} %param.4) | copy-start | bytes 6291460
  0.0 4.1 %copy-start.1 = (bf16[64,4096]{1,0:T(8,128)(2,1)S(1)}, bf16[64,4096]{1,0:T(8,128)(2,1)}, u32[]{:S(2)}) copy-start(bf16[64,4096]{1,0:T(8,128)(2,1)} %param.3) | copy-start | bytes 1572868
  0.0 12.5 %collective-permute-start = (bf16[64,4096]{1,0:T(8,128)(2,1)}, bf16[64,4096]{1,0:T(8,128)(2,1)S(1)}, u32[]{:S(2)}, u32[]{:S(2)}) collective-permute-start(bf16[64,4096]{1,0:T(8,128)(2,1)} %param.3), channel_id=1, source_target_pairs={{0,1},{1,2},{2,3},{3,0},{4,5},{5,6},{6,7},{7,4},{8,9},{9,10},{10,1... | collective-permute-start | bytes 1572872 | tf_op jit(solution)/shard_map/ppermute | solution.py:107
  0.5 15.5 %collective-permute-start.1 = (bf16[64,4096]{1,0:T(8,128)(2,1)}, bf16[64,4096]{1,0:T(8,128)(2,1)}, u32[]{:S(2)}, u32[]{:S(2)}) collective-permute-start(bf16[64,4096]{1,0:T(8,128)(2,1)} %param.3), channel_id=1, source_target_pairs={{0,3},{1,0},{2,1},{3,2},{4,7},{5,4},{6,5},{7,6},{8,11},{9,8},{10,9... | collective-permute-start | bytes 1572872 | tf_op jit(solution)/shard_map/ppermute | solution.py:110
  12.5 8.6 %collective-permute-start.2 = (bf16[64,4096]{1,0:T(8,128)(2,1)S(1)}, bf16[64,4096]{1,0:T(8,128)(2,1)S(1)}, u32[]{:S(2)}, u32[]{:S(2)}) collective-permute-start(bf16[64,4096]{1,0:T(8,128)(2,1)S(1)} %collective-permute-done), channel_id=1, source_target_pairs={{0,1},{1,2},{2,3},{3,0},{4,5},{5,6},{6,7},{7,4},{8,9},{9,10},{10,1... | collective-permute-start | bytes 1572872 | tf_op jit(solution)/shard_map/ppermute | solution.py:107
  24.3 5.7 %collective-permute-start.3 = (f32[256,5]{0,1:T(8,128)S(1)}, f32[256,5]{0,1:T(8,128)S(1)}, u32[]{:S(2)}, u32[]{:S(2)}) collective-permute-start(f32[256,5]{0,1:T(8,128)S(1)} %get-tuple-element.12), channel_id=1, source_target_pairs={{0,1},{1,2},{2,3},{3,4},{4,5},{5,6},{6,7},{7,8},{8,9},{9,10},{10,1... | collective-permute-start | bytes 15368 | tf_op jit(solution)/shard_map/ppermute | solution.py:20
  28.7 5.0 %collective-permute-start.4 = (f32[256,5]{0,1:T(8,128)S(1)}, f32[256,5]{0,1:T(8,128)S(1)}, u32[]{:S(2)}, u32[]{:S(2)}) collective-permute-start(f32[256,5]{0,1:T(8,128)S(1)} %get-tuple-element.13), channel_id=1, source_target_pairs={{1,0},{2,1},{3,2},{4,3},{5,4},{6,5},{7,6},{8,7},{9,8},{10,9},{11,1... | collective-permute-start | bytes 15368 | tf_op jit(solution)/shard_map/ppermute | solution.py:21
  33.8 4.9 %copy-start.2 = (s32[5]{0:T(128)S(1)}, s32[5]{0:T(128)}, u32[]{:S(2)}) copy-start(s32[5]{0:T(128)} %param.5) | copy-start | bytes 64
  34.4 23.5 %collective-permute-start.5 = (f32[256,114]{0,1:T(8,128)S(1)}, f32[256,114]{0,1:T(8,128)S(1)}, u32[]{:S(2)}, u32[]{:S(2)}) collective-permute-start(f32[256,114]{0,1:T(8,128)S(1)} %slice.220), channel_id=1, source_target_pairs={{0,1},{1,2},{2,3},{3,4},{4,5},{5,6},{6,7},{7,8},{8,9},{9,10},{10,1... | collective-permute-start | bytes 350216 | tf_op jit(solution)/shard_map/ppermute | solution.py:29
